TPU v7x, 1024 devices: a whole 8x8x8 slice. The times are simulated.
1024 devices in a mesh: tower: 32 (over x, y_lo), intra: 32 (over y_hi, z, core).
Axes of the slice: x: 8, y: 8 (y_hi: 2, y_lo: 4; y = y_hi * 4 + y_lo), z: 8, core: 2. Of those that a mesh axis runs over, the one named last changes fastest.
Arguments:
- embeddings: bfloat16 [8192, 131072], P(None, ('tower', 'intra')), may hold values from -6 to 6
- feature_assign: int32 [32, 32], P('tower'), may hold values from 0 to 31, each once within a row
- sample_owner: int32 [8192], replicated, may hold values from 0 to 8191, each once
- first_weight: bfloat16 [64, 2048, 1024], P('tower'), may hold values from -0.125 to 0.125
- first_bias: float32 [64, 1024], P('tower'), may hold values from -3 to 3
- tower_weight: bfloat16 [64, 1024, 256], P('tower'), may hold values from -0.1875 to 0.1875
- tower_bias: float32 [64, 256], P('tower'), may hold values from -3 to 3
- proj_weight: bfloat16 [128, 128], replicated, may hold values from -0.5 to 0.5
Outputs:
- interaction: bfloat16 [8192, 128, 128], P(('tower', 'intra'))
Inputs may be any that keep to these rules, and one draw needn't show every extreme that they name: `feature_assign`: each row is a permutation of 0 to 31. `sample_owner`: a permutation of 0 to 8191.
All inputs are finite; a program needn't handle non-finite values.
Results may differ from a plain program's by a relative error of at most 0.0034.
Values may be sent and summed in bfloat16 or wider, within the bound.
A program may use at most 64 MiB of HBM per device.

v0:
```python
import jax
import jax.numpy as jnp
from jax import lax
from jax.sharding import PartitionSpec as P

EDIM = 128
TOW_DEV = 2
TIN = 2048
TVEC = 2
FPT = 32


def shards(
    embeddings,
    feature_assign,
    sample_owner,
    first_weight,
    first_bias,
    tower_weight,
    tower_bias,
    proj_weight,
):
    tower_count = lax.axis_size("tower")
    intra_count = lax.axis_size("intra")
    samples = embeddings.shape[0]
    per_device = samples // (tower_count * intra_count)
    block_rows = per_device * tower_count
    sample_order = (
        sample_owner.reshape(tower_count, intra_count, per_device).transpose(1, 0, 2).reshape(-1)
    )
    ordered = jnp.take(embeddings, sample_order, axis=0)
    outgoing = ordered.reshape(intra_count, block_rows, embeddings.shape[1])
    assign_row = feature_assign[0]
    received = lax.all_to_all(outgoing, "intra", split_axis=0, concat_axis=2, tiled=True)
    count = received.shape[1]
    features = received.reshape(count, FPT, EDIM)
    features = jnp.take(features, assign_row, axis=1)
    inputs = features.reshape(count, TOW_DEV, TIN)
    hidden = jnp.einsum("nkc,kch->nkh", inputs, first_weight, preferred_element_type=jnp.float32)
    hidden = jnp.maximum(hidden + first_bias[None, :, :], 0.0).astype(jnp.bfloat16)
    result = jnp.einsum("nkh,kho->nko", hidden, tower_weight, preferred_element_type=jnp.float32)
    result = result + tower_bias[None, :, :]
    vectors = jnp.maximum(result, 0.0).astype(jnp.bfloat16).reshape(count, TOW_DEV * TVEC, EDIM)
    owned = lax.all_to_all(vectors, "tower", split_axis=0, concat_axis=1, tiled=True)
    gram_matrix = (
        jnp.einsum("pie,pje->pij", owned, owned, preferred_element_type=jnp.float32) / EDIM
    )
    result = jnp.einsum(
        "pij,je->pie", gram_matrix, proj_weight.astype(jnp.float32), precision=lax.Precision.HIGHEST
    )
    return result.astype(jnp.bfloat16)


def solution(mesh):
    return jax.shard_map(
        shards,
        mesh=mesh,
        in_specs=(
            P(None, ("tower", "intra")),
            P("tower", None),
            P(),
            P("tower", None, None),
            P("tower", None),
            P("tower", None, None),
            P("tower", None),
            P(),
        ),
        out_specs=P(("tower", "intra"), None, None),
        check_vma=False,
    )
```

profile of v0, /device:TPU:1, one launch (start us, length us, event | category | flops | bytes accessed | tf_op | source)
XLA Modules:
  0.0 153.3 jit_solution(18325466685239936788)
XLA Ops:
  0.0 1.2 reshape.98
  1.2 0.3 copy.28
  1.5 0.2 copy.26
  1.7 0.3 reshape.100
  2.1 0.1 copy.27
  2.2 29.4 %gather_fusion = bf16[8192,128]{1,0:T(8,128)(2,1)} fusion(bf16[8192,128]{1,0:T(8,128)(2,1)S(1)} %copy-done, s32[8192]{0:T(1024)S(1)} %broadcast_clamp_fusion), kind=kCustom, calls=%fused_computation | custom fusion | bytes 4227072 | tf_op jit(solution)/shard_map/jit(_take)/gather | solution.py:31
  31.6 4.4 %broadcast_select_fusion = bf16[32,256,128]{2,1,0:T(8,128)(2,1)} fusion(bf16[32,256,128]{2,1,0:T(8,128)(2,1)} %bitcast.45, pred[32,256]{1,0:T(8,128)(4,1)S(1)} %copy.27), kind=kLoop, calls=%fused_computation.4 | loop fusion | flops 1048576 | bytes 4202496 | tf_op jit(solution)/shard_map/jit(_take)/select_n | solution.py:31
  36.0 24.2 %all-to-all-start = ((bf16[32,256,128]{2,1,0:T(8,128)(2,1)}), bf16[32,256,128]{2,1,0:T(8,128)(2,1)}, u32[]{:S(2)}, u32[]{:S(2)}) async-start(bf16[32,256,128]{2,1,0:T(8,128)(2,1)} %broadcast_select_fusion), calls=%async_computation | async-start | bytes 4194304 | tf_op jit(solution)/shard_map/all_to_all | solution.py:34
  60.3 0.5 broadcast.83
  60.8 0.0 copy-done.4
  60.8 0.7 reduce.3
  61.4 0.1 squeeze.5
  61.5 0.1 broadcast_bitcast_fusion
  61.7 49.8 %all-to-all-done = bf16[32,256,128]{2,1,0:T(8,128)(2,1)} async-done(((bf16[32,256,128]{2,1,0:T(8,128)(2,1)}), bf16[32,256,128]{2,1,0:T(8,128)(2,1)}, u32[]{:S(2)}, u32[]{:S(2)}) %all-to-all-start) | async-done | bytes 2097184 | tf_op jit(solution)/shard_map/all_to_all | solution.py:34
  111.4 3.7 %gather_fusion.1 = bf16[32,256,128]{2,1,0:T(8,128)(2,1)} fusion(bf16[256,32,128]{2,0,1:T(8,128)(2,1)} %bitcast.6, s32[1024]{0:T(1024)S(1)} %pad_clamp_fusion), kind=kCustom, calls=%fused_computation.1 | custom fusion | bytes 4194432 | tf_op jit(solution)/shard_map/jit(_take)/gather | solution.py:37
  115.2 4.1 %copy.29 = bf16[256,32,128]{0,2,1:T(8,128)(2,1)} copy(bf16[256,32,128]{2,0,1:T(8,128)(2,1)} %bitcast.46) | data formatting | bytes 4194304 | tf_op jit(solution)/shard_map/jit(_take)/gather | solution.py:37
  119.2 2.9 %bitcast_select_fusion = bf16[256,2,2048]{0,2,1:T(8,128)(2,1)} fusion(pred[2,2048]{1,0:T(4,128)(4,1)S(1)} %bitcast.54, bf16[256,2,2048]{0,2,1:T(8,128)(2,1)} %bitcast.47), kind=kLoop, calls=%fused_computation.2 | loop fusion | flops 1048576 | bytes 4198400 | tf_op jit(solution)/shard_map/jit(_take)/select_n | solution.py:37
  122.1 6.9 %fusion.2 = bf16[2,256,256]{1,2,0:T(8,128)(2,1)S(1)} fusion(bf16[2,1024,256]{2,1,0:T(8,128)(2,1)} %param.13, bf16[256,2,2048]{0,2,1:T(8,128)(2,1)} %bitcast_select_fusion, bf16[2,2048,1024]{2,1,0:T(8,128)(2,1)} %param.11, f32[2,1024]{1,0:T(2,128)S(1)} %copy-done.2, f32[2,256]{1,0:T(2,128)S(1)} %copy-done.3), kind=kOutput, calls=%fused_computation.9 | convolution fusion | flops 2417885184 | bytes 11806720 | tf_op jit(solution)/shard_map/nkh,kho->nko/dot_general | solution.py:41
  129.1 0.0 copy-start.1
  129.1 0.2 copy.32
  129.3 22.6 %all_to_all.33 = bf16[256,4,128]{2,1,0:T(4,128)(2,1)S(1)} all-to-all(bf16[256,4,128]{2,1,0:T(4,128)(2,1)S(1)} %copy.32), channel_id=1, replica_groups=mesh['tower'=32,'intra'=32] {'tower'}, dimensions={0} | all-to-all | bytes 524288 | tf_op jit(solution)/shard_map/all_to_all | solution.py:44
  151.9 0.3 convolution_multiply_fusion
  152.2 0.0 copy-done.1
  152.2 1.1 convolution_convert_fusion
  (16 shorter events, 0.2 us)
Async XLA Ops:
  0.0 2.2 %copy-start = (bf16[8192,128]{1,0:T(8,128)(2,1)S(1)}, bf16[8192,128]{1,0:T(8,128)(2,1)}, u32[]{:S(2)}) copy-start(bf16[8192,128]{1,0:T(8,128)(2,1)} %param.8) | copy-start | bytes 6291460
  36.0 24.8 %copy-start.4 = (s32[1,32]{1,0:T(1,128)S(1)}, s32[1,32]{1,0:T(1,128)}, u32[]{:S(2)}) copy-start(s32[1,32]{1,0:T(1,128)} %param.9) | copy-start | bytes 388
  36.0 75.4 %all-to-all-start = ((bf16[32,256,128]{2,1,0:T(8,128)(2,1)}), bf16[32,256,128]{2,1,0:T(8,128)(2,1)}, u32[]{:S(2)}, u32[]{:S(2)}) async-start(bf16[32,256,128]{2,1,0:T(8,128)(2,1)} %broadcast_select_fusion), calls=%async_computation | async-start | bytes 4194304 | tf_op jit(solution)/shard_map/all_to_all | solution.py:34
  119.2 2.9 %copy-start.2 = (f32[2,1024]{1,0:T(2,128)S(1)}, f32[2,1024]{1,0:T(2,128)}, u32[]{:S(2)}) copy-start(f32[2,1024]{1,0:T(2,128)} %param.12) | copy-start | bytes 24580
  119.2 2.9 %copy-start.3 = (f32[2,256]{1,0:T(2,128)S(1)}, f32[2,256]{1,0:T(2,128)}, u32[]{:S(2)}) copy-start(f32[2,256]{1,0:T(2,128)} %param.14) | copy-start | bytes 6148
  129.1 23.2 %copy-start.1 = (bf16[128,128]{1,0:T(8,128)(2,1)S(1)}, bf16[128,128]{1,0:T(8,128)(2,1)}, u32[]{:S(2)}) copy-start(bf16[128,128]{1,0:T(8,128)(2,1)} %param.15) | copy-start | bytes 98308
where the time goes:
time: 156 us; the launch traced here: 153 us
  waiting for transfers between devices  49.8 us (32%)
  local copies, waits for them, and re-layouts  40.2 us (26%)
  starting transfers between devices  24.2 us (16%)
  blocking collectives  22.6 us (14%)
  matrix products  8.33 us (5%)
  other arithmetic  8.08 us (5%)
    all_to_all x1, waiting for transfers between devices, shards(): lax.all_to_all(outgoing, 'intra', split_axis=0, concat_axis=2, tiled=True)  49.8 us
    gather x1, local copies, waits for them, and re-layouts, shards(): ordered = jnp.take(embeddings, sample_order, axis=0)  29.4 us
    all_to_all x1, starting transfers between devices, shards(): lax.all_to_all(outgoing, 'intra', split_axis=0, concat_axis=2, tiled=True)  24.2 us
    all_to_all x1, blocking collectives, shards(): lax.all_to_all(vectors, 'tower', split_axis=0, concat_axis=1, tiled=True)  22.6 us
    gather x2, local copies, waits for them, and re-layouts, shards(): features = jnp.take(features, assign_row, axis=1)  7.77 us
    dot_general x1, matrix products, shards(): jnp.einsum('nkh,kho->nko', hidden, tower_weight, preferred_element_type=j...  6.94 us
    select_n x2, other arithmetic, shards(): ordered = jnp.take(embeddings, sample_order, axis=0)  4.42 us
  transfers between devices with their start and end apart: 1, of which 1 were waited for; matrix products, arithmetic and copies ran while one was open for 1% of the time, Pallas kernels for 0%

commit v1 on v0

v1 whole, which is shorter than its diff:
```python
import functools

import jax
import jax.numpy as jnp
from jax import lax
from jax.experimental import pallas as pl
from jax.experimental.pallas import tpu as pltpu
from jax.sharding import PartitionSpec as P

EDIM = 128
TOW_DEV = 2
TFEAT = 16
TIN = 2048
HID = 1024
TOUT = 256
SD = 8
QV = 4
N_TOWER = 32
N_INTRA = 32
SAMPLES = 8192
CHUNKS = ((4, 5), (3, 6), (2, 7), (1, 0))
NCH = len(CHUNKS)
POS = 8
ROWS = POS * SD
EMB_PARTS = 4
MESH = pl.DeviceIdType.MESH
BF16 = jnp.bfloat16
F32 = jnp.float32


def kernel(
    owner, assign, emb_hbm, w1_hbm, b1, w2_hbm, b2, proj, out,
    emb_b, emb_f, stage, r0, r1, r2, r3, w1, w2, rows_f, x, hid, send, own, own_f, out_f, proj_f,
    emb_sem, w_sem, send_sem, recv_sem, send2_sem, recv2_sem,
):
    recv = (r0, r1, r2, r3)
    tower = lax.axis_index("tower")
    me = lax.axis_index("intra")
    tx, ty = tower // 4, tower % 4
    y_hi, z, core = me // 16, (me // 2) % 8, me % 2

    part = SAMPLES // EMB_PARTS
    emb_copies = [
        pltpu.make_async_copy(
            emb_hbm.at[pl.ds(i * part, part)], emb_b.at[pl.ds(i * part, part)], emb_sem.at[i]
        )
        for i in range(EMB_PARTS)
    ]
    for copy in emb_copies:
        copy.start()

    barrier = pltpu.get_barrier_semaphore()

    @pl.loop(1, N_INTRA)
    def _(k):
        pl.semaphore_signal(
            barrier, inc=1, device_id={"intra": lax.rem(me + k, N_INTRA)}, device_id_type=MESH
        )
        pl.semaphore_signal(
            barrier, inc=1, device_id={"tower": lax.rem(tower + k, N_TOWER)}, device_id_type=MESH
        )

    for i, copy in enumerate(emb_copies):
        copy.wait()
        emb_f[pl.ds(i * part, part), :] = emb_b[pl.ds(i * part, part), :].astype(F32)

    w_copies = [
        pltpu.make_async_copy(w1_hbm, w1, w_sem.at[0]),
        pltpu.make_async_copy(w2_hbm, w2, w_sem.at[1]),
    ]
    for copy in w_copies:
        copy.start()

    def towers_of(c):
        return [
            ((tx + dx) % 8) * 4 + (ty + dy) % 4 for dx in CHUNKS[c] for dy in range(4)
        ]

    def peer_of(k):
        kk = 7 - k % 8
        odd = kk % 2
        dz = odd * ((kk + 1) // 2) + (1 - odd) * (8 - kk // 2)
        dy = 1 - (k // 8) % 2
        dc = 1 - k // 16
        return ((y_hi + dy) % 2) * 16 + ((z + dz) % 8) * 2 + (core + dc) % 2

    def gather(targets, peer):
        for pos in range(POS):
            base = (targets[pos] * N_INTRA + peer) * SD
            for r in range(SD):
                rows_f[pl.ds(pos * SD + r, 1), :] = emb_f[pl.ds(owner[base + r], 1), :]
        return rows_f[...].astype(BF16)

    pl.semaphore_wait(barrier, (N_INTRA - 1) + (N_TOWER - 1))

    for c in range(NCH):
        targets = towers_of(c)

        def copy_of(k, c=c):
            return pltpu.make_async_remote_copy(
                src_ref=stage.at[c, k],
                dst_ref=recv[c].at[me],
                send_sem=send_sem.at[c],
                recv_sem=recv_sem.at[c],
                device_id={"intra": peer_of(k)},
                device_id_type=MESH,
            )

        @pl.loop(0, N_INTRA - 1)
        def _(k, c=c, targets=targets, copy_of=copy_of):
            stage[c, k] = gather(targets, peer_of(k))

            @pl.when(k > 0)
            def _():
                copy_of(k - 1).start()

        recv[c][me] = gather(targets, me)
        copy_of(N_INTRA - 2).start()

    for copy in w_copies:
        copy.wait()

    for c in range(NCH):
        targets = towers_of(c)
        arrived = recv[c].at[pl.ds(0, N_INTRA - 1)]
        pltpu.make_async_copy(arrived, arrived, recv_sem.at[c]).wait()
        for m in range(TOW_DEV):
            for s in range(TFEAT):
                x[m, :, s * EDIM : (s + 1) * EDIM] = recv[c][assign[0, m * TFEAT + s]]
        result = []
        for m in range(TOW_DEV):
            for n in range(HID // 256):
                cols = slice(n * 256, (n + 1) * 256)
                total = jnp.dot(x[m], w1[m, :, cols], preferred_element_type=F32)
                hid[m, :, cols] = jnp.maximum(total + b1[pl.ds(m, 1), cols], 0.0).astype(BF16)
            total = jnp.dot(hid[m], w2[m], preferred_element_type=F32)
            result.append(jnp.maximum(total + b2[pl.ds(m, 1), :], 0.0))
        for pos in range(POS):
            rows = slice(pos * SD, (pos + 1) * SD)
            block = jnp.concatenate(
                [result[q // 2][rows, (q % 2) * EDIM : (q % 2 + 1) * EDIM] for q in range(QV)], axis=0
            )
            if CHUNKS[c][pos // 4] == 0 and pos % 4 == 0:
                own[tower] = block.astype(BF16)
            else:
                send[c, pos] = block.astype(BF16)
        for pos in range(POS):
            if CHUNKS[c][pos // 4] == 0 and pos % 4 == 0:
                continue
            pltpu.make_async_remote_copy(
                src_ref=send.at[c, pos],
                dst_ref=own.at[tower],
                send_sem=send2_sem,
                recv_sem=recv2_sem,
                device_id={"tower": targets[pos]},
                device_id_type=MESH,
            ).start()

    proj_f[...] = proj[...].astype(F32)
    weight = jnp.concatenate([proj_f[pl.ds(q, N_TOWER, stride=QV), :] for q in range(QV)], axis=0)
    weight = weight.astype(BF16)

    arrived = own.at[pl.ds(0, N_TOWER - 1)]
    pltpu.make_async_copy(arrived, arrived, recv2_sem).wait()

    own_f[...] = own[...].astype(F32).reshape(N_TOWER * QV * SD, EDIM)
    for r in range(SD):
        vectors = jnp.concatenate(
            [own_f[pl.ds(q * SD + r, N_TOWER, stride=QV * SD), :] for q in range(QV)], axis=0
        ).astype(BF16)
        gram = lax.dot_general(
            vectors, vectors, (((1,), (1,)), ((), ())), preferred_element_type=F32
        ) * (1.0 / EDIM)
        high = gram.astype(BF16)
        low = (gram - high.astype(F32)).astype(BF16)
        result = jnp.dot(high, weight, preferred_element_type=F32)
        result = result + jnp.dot(low, weight, preferred_element_type=F32)
        for q in range(QV):
            out_f[r, pl.ds(q, N_TOWER, stride=QV), :] = result[q * N_TOWER : (q + 1) * N_TOWER, :]
        out[r] = out_f[r].astype(BF16)

    for c in range(NCH):
        left = stage.at[c, pl.ds(0, N_INTRA - 1)]
        pltpu.make_async_copy(left, left, send_sem.at[c]).wait()
    left = own.at[pl.ds(0, N_TOWER - 1)]
    pltpu.make_async_copy(left, left, send2_sem).wait()


def shards(
    embeddings,
    feature_assign,
    sample_owner,
    first_weight,
    first_bias,
    tower_weight,
    tower_bias,
    proj_weight,
):
    vmem = pl.BlockSpec(memory_space=pltpu.VMEM)
    smem = pl.BlockSpec(memory_space=pltpu.SMEM)
    hbm = pl.BlockSpec(memory_space=pl.ANY)
    dma = pltpu.SemaphoreType.DMA
    recv = [pltpu.VMEM((N_INTRA, ROWS, EDIM), BF16) for _ in range(NCH)]
    return pl.pallas_call(
        kernel,
        out_shape=jax.ShapeDtypeStruct((SD, N_TOWER * QV, EDIM), BF16),
        in_specs=[smem, smem, hbm, hbm, vmem, hbm, vmem, vmem],
        out_specs=vmem,
        scratch_shapes=[
            pltpu.VMEM((SAMPLES, EDIM), BF16),
            pltpu.VMEM((SAMPLES, EDIM), F32),
            pltpu.VMEM((NCH, N_INTRA, ROWS, EDIM), BF16),
            *recv,
            pltpu.VMEM((TOW_DEV, TIN, HID), BF16),
            pltpu.VMEM((TOW_DEV, HID, TOUT), BF16),
            pltpu.VMEM((ROWS, EDIM), F32),
            pltpu.VMEM((TOW_DEV, ROWS, TIN), BF16),
            pltpu.VMEM((TOW_DEV, ROWS, HID), BF16),
            pltpu.VMEM((NCH, POS, QV * SD, EDIM), BF16),
            pltpu.VMEM((N_TOWER, QV * SD, EDIM), BF16),
            pltpu.VMEM((N_TOWER * QV * SD, EDIM), F32),
            pltpu.VMEM((SD, N_TOWER * QV, EDIM), F32),
            pltpu.VMEM((N_TOWER * QV, EDIM), F32),
            dma((EMB_PARTS,)),
            dma((2,)),
            dma((NCH,)),
            dma((NCH,)),
            dma,
            dma,
        ],
        compiler_params=pltpu.CompilerParams(
            collective_id=0, has_side_effects=True, vmem_limit_bytes=48 * 1024 * 1024
        ),
        name="towers",
    )(
        sample_owner,
        feature_assign,
        embeddings,
        first_weight,
        first_bias,
        tower_weight,
        tower_bias,
        proj_weight,
    )


def solution(mesh):
    return jax.shard_map(
        shards,
        mesh=mesh,
        in_specs=(
            P(None, ("tower", "intra")),
            P("tower", None),
            P(),
            P("tower", None, None),
            P("tower", None),
            P("tower", None, None),
            P("tower", None),
            P(),
        ),
        out_specs=P(("tower", "intra"), None, None),
        check_vma=False,
    )
```

time: 156 us -> 94 us (0.60)
  Pallas kernels: 0 us -> 85.4 us
  waiting for transfers between devices: 49.8 us -> 0 us
  local copies, waits for them, and re-layouts: 40.2 us -> 7.07 us
  starting transfers between devices: 24.2 us -> 0 us
  blocking collectives: 22.6 us -> 0 us
  matrix products: 8.33 us -> 0 us
  other arithmetic: 8.08 us -> 0 us
    pallas_call x0 -> x1, Pallas kernels: none -> 85.4 us  [shards(): pl.pallas_call(kernel, out_shape=jax.ShapeDtypeStruct((SD, N_TOWER * QV,...]
    all_to_all x1 -> x0, waiting for transfers between devices: 49.8 us -> none  [shards(): lax.all_to_all(outgoing, 'intra', split_axis=0, concat_axis=2, tiled=True)]
    gather x3 -> x0, local copies, waits for them, and re-layouts: 37.2 us -> none  [the longest x1 29.4 us: shards(): ordered = jnp.take(embeddings, sample_order, axis=0)]
    all_to_all x1 -> x0, starting transfers between devices: 24.2 us -> none  [shards(): lax.all_to_all(outgoing, 'intra', split_axis=0, concat_axis=2, tiled=True)]
    all_to_all x1 -> x0, blocking collectives: 22.6 us -> none  [shards(): lax.all_to_all(vectors, 'tower', split_axis=0, concat_axis=1, tiled=True)]
    dot_general x3 -> x0, matrix products: 8.33 us -> none  [the longest x1 6.94 us: shards(): jnp.einsum('nkh,kho->nko', hidden, tower_weight, preferred_element_type=j...]
    select_n x4 -> x0, other arithmetic: 7.34 us -> none  [the longest x2 4.42 us: shards(): ordered = jnp.take(embeddings, sample_order, axis=0)]
    unnamed x13 -> x15, local copies, waits for them, and re-layouts: 0.63 us -> 7.07 us
  transfers between devices with their start and end apart: 1 -> 0, of which waited for: 1 -> 0; matrix products, arithmetic and copies ran while one was open for 1% -> 0% of each run, Pallas kernels for 0% -> 0%
where the time goes in v1:
time: 94 us; the launch traced here: 92.5 us
  Pallas kernels  85.4 us (91%)
  local copies, waits for them, and re-layouts  7.07 us (8%)
    pallas_call x1, Pallas kernels, shards(): pl.pallas_call(kernel, out_shape=jax.ShapeDtypeStruct((SD, N_TOWER * QV,...  85.4 us
    unnamed x15, local copies, waits for them, and re-layouts  7.07 us

profile of v1, /device:TPU:1, one launch (start us, length us, event | category | flops | bytes accessed | tf_op | source)
XLA Modules:
  0.0 92.5 jit_solution(11939565030925227164)
XLA Ops:
  0.0 0.0 copy-start
  0.0 1.6 %copy-done = bf16[8192,128]{1,0:T(8,128)(2,1)S(1)} copy-done((bf16[8192,128]{1,0:T(8,128)(2,1)S(1)}, bf16[8192,128]{1,0:T(8,128)(2,1)}, u32[]{:S(2)}) %copy-start) | copy-done | bytes 2097176
  1.6 0.0 copy-start.1
  1.6 1.2 %copy-done.1 = bf16[2,1024,256]{2,1,0:T(8,128)(2,1)S(1)} copy-done((bf16[2,1024,256]{2,1,0:T(8,128)(2,1)S(1)}, bf16[2,1024,256]{2,1,0:T(8,128)(2,1)}, u32[]{:S(2)}) %copy-start.1) | copy-done | bytes 1048600
  2.8 0.0 copy-start.2
  2.8 0.8 copy-done.2
  3.6 0.0 copy-start.3
  3.6 0.8 copy-done.3
  4.3 0.0 copy-start.4
  4.3 0.7 copy-done.4
  5.0 0.0 copy-start.5
  5.0 0.7 copy-done.5
  5.7 0.0 copy-start.6
  5.7 0.7 copy-done.6
  6.4 85.4 %towers.1 = bf16[8,128,128]{2,1,0:T(8,128)(2,1)S(1)} custom-call(s32[8192]{0:T(1024)S(1)} %copy-done.2, s32[1,32]{1,0:T(1,128)S(1)} %copy-done.6, bf16[8192,128]{1,0:T(8,128)(2,1)S(1)} %copy-done, bf16[2,2048,1024]{2,1,0:T(8,128)(2,1)} %w1_hbm.1, f32[2,1024]{1,0:T(2,128)S(1)} %copy-done.4, bf16[2,1024,256]{2,1,0:T(8,128)(2,1)S(1)} %copy-done.1, ...), custom_call_target="tpu_custom_call" | custom-call | tf_op jit(solution)/shard_map/towers/pallas_call | solution.py:204
  91.8 0.7 copy.10
Async XLA Ops:
  0.0 1.6 %copy-start = (bf16[8192,128]{1,0:T(8,128)(2,1)S(1)}, bf16[8192,128]{1,0:T(8,128)(2,1)}, u32[]{:S(2)}) copy-start(bf16[8192,128]{1,0:T(8,128)(2,1)} %emb_hbm.1) | copy-start | bytes 6291460
  1.6 1.2 %copy-start.1 = (bf16[2,1024,256]{2,1,0:T(8,128)(2,1)S(1)}, bf16[2,1024,256]{2,1,0:T(8,128)(2,1)}, u32[]{:S(2)}) copy-start(bf16[2,1024,256]{2,1,0:T(8,128)(2,1)} %w2_hbm.1) | copy-start | bytes 3145732
  2.8 0.8 copy-start.2
  3.6 0.8 copy-start.3
  4.3 0.7 copy-start.4
  5.0 0.7 copy-start.5
  5.7 0.7 copy-start.6

commit v2 on v1

v2 whole, which is shorter than its diff:
```python
import jax
import jax.numpy as jnp
from jax import lax
from jax.experimental import pallas as pl
from jax.experimental.pallas import tpu as pltpu
from jax.sharding import PartitionSpec as P

EDIM = 128
TOW_DEV = 2
TFEAT = 16
TIN = 2048
HID = 1024
TOUT = 256
SD = 8
QV = 4
N_TOWER = 32
N_INTRA = 32
SAMPLES = 8192
CHUNKS = ((4, 5), (3, 6), (2, 7), (1,), (0,))
NCH = len(CHUNKS)
RUN = 4
ROWS = tuple(len(offsets) * RUN * SD for offsets in CHUNKS)
FIRST = tuple(RUN * sum(len(offsets) for offsets in CHUNKS[:c]) for c in range(NCH))
EMB_PARTS = 4
AHEAD = 16
MESH = pl.DeviceIdType.MESH
BF16 = jnp.bfloat16
F32 = jnp.float32


def kernel(
    owner_hbm, assign_hbm, emb_hbm, w1_hbm, b1_hbm, w2_hbm, b2_hbm, proj_hbm, out, *scratch
):
    stage, recv = scratch[:NCH], scratch[NCH : 2 * NCH]
    (
        owner, assign, b1, b2, proj, emb_b, emb_f, w1, w2, rows_f, x, hid, send, own, own_f, out_f, proj_f,
        emb_sem, table_sem, w_sem, send_sem, recv_sem, send2_sem, recv2_sem,
    ) = scratch[2 * NCH :]
    tower = lax.axis_index("tower")
    me = lax.axis_index("intra")
    tx = tower // RUN
    y = (me // 16) * RUN + tower % RUN
    z, core = (me // 2) % 8, me % 2

    part = SAMPLES // EMB_PARTS
    emb_copies = [
        pltpu.make_async_copy(
            emb_hbm.at[pl.ds(i * part, part)], emb_b.at[pl.ds(i * part, part)], emb_sem.at[i]
        )
        for i in range(EMB_PARTS)
    ]
    owner_copy = pltpu.make_async_copy(owner_hbm, owner, table_sem)
    others = ((assign_hbm, assign), (b1_hbm, b1), (b2_hbm, b2), (proj_hbm, proj), (w2_hbm, w2), (w1_hbm, w1))
    w_copies = [
        pltpu.make_async_copy(source, target, w_sem.at[i]) for i, (source, target) in enumerate(others)
    ]
    owner_copy.start()
    for copy in emb_copies:
        copy.start()

    barrier = pltpu.get_barrier_semaphore()

    def place(px, py, pz, pcore):
        return {"tower": px * RUN + py % RUN, "intra": (py // RUN) * 16 + pz * 2 + pcore}

    def y_step(dx, step):
        return (step % 2) * (2 - step) + (step // 2) * (1 - step % 2) * (2 - 4 * (dx % 2))

    @pl.loop(1, N_INTRA)
    def _(k):
        pl.semaphore_signal(
            barrier, inc=1, device_id={"intra": lax.rem(me + k, N_INTRA)}, device_id_type=MESH
        )
        dx = k // RUN
        sender = place((tx + 8 - dx) % 8, (y + 8 - y_step(dx, k % RUN)) % 8, z, core)
        pl.semaphore_signal(barrier, inc=1, device_id=sender, device_id_type=MESH)

    for i, copy in enumerate(emb_copies):
        copy.wait()
        emb_f[pl.ds(i * part, part), :] = emb_b[pl.ds(i * part, part), :].astype(F32)
    for copy in w_copies:
        copy.start()
    owner_copy.wait()

    def steps_of(c):
        return [(dx, y_step(dx, step)) for dx in CHUNKS[c] for step in range(RUN)]

    def peer_of(k):
        kk = 7 - k % 8
        odd = kk % 2
        dz = odd * ((kk + 1) // 2) + (1 - odd) * (8 - kk // 2)
        dy = 1 - (k // 8) % 2
        dc = 1 - k // 16
        return tx, (y + RUN * dy) % 8, (z + dz) % 8, (core + dc) % 2

    def gather(steps, peer):
        rows = len(steps) * SD
        px, py, pz, pcore = peer
        for pos, (dx, dy) in enumerate(steps):
            target = place((px + dx) % 8, (py + 8 + dy) % 8, pz, pcore)
            base = (target["tower"] * N_INTRA + target["intra"]) * SD
            for r in range(SD):
                rows_f[pl.ds(pos * SD + r, 1), :] = emb_f[pl.ds(owner[base + r], 1), :]
        return rows_f[pl.ds(0, rows), :].astype(BF16)

    for c in range(NCH):
        steps = steps_of(c)

        def copy_of(k, c=c):
            return pltpu.make_async_remote_copy(
                src_ref=stage[c].at[k],
                dst_ref=recv[c].at[me],
                send_sem=send_sem.at[c],
                recv_sem=recv_sem.at[c],
                device_id=place(*peer_of(k)),
                device_id_type=MESH,
            )

        if c == 0:

            @pl.loop(0, AHEAD)
            def _(k, steps=steps):
                stage[0][k] = gather(steps, peer_of(k))

            pl.semaphore_wait(barrier, (N_INTRA - 1) + (N_TOWER - 1))

            @pl.loop(0, AHEAD - 1)
            def _(k, copy_of=copy_of):
                copy_of(k).start()

        begin = AHEAD if c == 0 else 0

        @pl.loop(begin, N_INTRA - 1)
        def _(k, c=c, steps=steps, copy_of=copy_of):
            stage[c][k] = gather(steps, peer_of(k))

            @pl.when(k > 0)
            def _():
                copy_of(k - 1).start()

        recv[c][me] = gather(steps, (tx, y, z, core))
        copy_of(N_INTRA - 2).start()

    for copy in w_copies:
        copy.wait()

    proj_f[...] = proj[...].astype(F32)
    weight = jnp.concatenate([proj_f[pl.ds(q, N_TOWER, stride=QV), :] for q in range(QV)], axis=0)
    proj[...] = weight.astype(BF16)

    for c in range(NCH):
        steps = steps_of(c)
        rows = ROWS[c]
        arrived = recv[c].at[pl.ds(0, N_INTRA - 1)]
        pltpu.make_async_copy(arrived, arrived, recv_sem.at[c]).wait()
        for m in range(TOW_DEV):
            for s in range(TFEAT):
                x[m, 0:rows, s * EDIM : (s + 1) * EDIM] = recv[c][assign[0, m * TFEAT + s]]
        result = []
        for m in range(TOW_DEV):
            for n in range(HID // 256):
                cols = slice(n * 256, (n + 1) * 256)
                total = jnp.dot(x[m, 0:rows, :], w1[m, :, cols], preferred_element_type=F32)
                hid[m, 0:rows, cols] = jnp.maximum(total + b1[pl.ds(m, 1), cols], 0.0).astype(BF16)
            total = jnp.dot(hid[m, 0:rows, :], w2[m], preferred_element_type=F32)
            result.append(jnp.maximum(total + b2[pl.ds(m, 1), :], 0.0))
        copies = []
        for pos, (dx, dy) in enumerate(steps):
            block = jnp.concatenate(
                [
                    result[q // 2][pos * SD : (pos + 1) * SD, (q % 2) * EDIM : (q % 2 + 1) * EDIM]
                    for q in range(QV)
                ],
                axis=0,
            ).astype(BF16)
            if (dx, dy) == (0, 0):
                own[tower] = block
                continue
            slot = FIRST[c] + pos
            send[slot] = block
            copies.append(
                pltpu.make_async_remote_copy(
                    src_ref=send.at[slot],
                    dst_ref=own.at[tower],
                    send_sem=send2_sem,
                    recv_sem=recv2_sem,
                    device_id=place((tx + dx) % 8, (y + 8 + dy) % 8, z, core),
                    device_id_type=MESH,
                )
            )
        for copy in copies:
            copy.start()

    arrived = own.at[pl.ds(0, N_TOWER - 1)]
    pltpu.make_async_copy(arrived, arrived, recv2_sem).wait()

    own_f[...] = own[...].astype(F32).reshape(N_TOWER * QV * SD, EDIM)
    weight = proj[...]
    for r in range(SD):
        vectors = jnp.concatenate(
            [own_f[pl.ds(q * SD + r, N_TOWER, stride=QV * SD), :] for q in range(QV)], axis=0
        ).astype(BF16)
        gram = lax.dot_general(
            vectors, vectors, (((1,), (1,)), ((), ())), preferred_element_type=F32
        ) * (1.0 / EDIM)
        high = gram.astype(BF16)
        low = (gram - high.astype(F32)).astype(BF16)
        result = jnp.dot(high, weight, preferred_element_type=F32)
        result = result + jnp.dot(low, weight, preferred_element_type=F32)
        for q in range(QV):
            out_f[r, pl.ds(q, N_TOWER, stride=QV), :] = result[q * N_TOWER : (q + 1) * N_TOWER, :]
        out[r] = out_f[r].astype(BF16)

    for c in range(NCH):
        left = stage[c].at[pl.ds(0, N_INTRA - 1)]
        pltpu.make_async_copy(left, left, send_sem.at[c]).wait()
    left = own.at[pl.ds(0, N_TOWER - 1)]
    pltpu.make_async_copy(left, left, send2_sem).wait()


def shards(
    embeddings,
    feature_assign,
    sample_owner,
    first_weight,
    first_bias,
    tower_weight,
    tower_bias,
    proj_weight,
):
    vmem = pl.BlockSpec(memory_space=pltpu.VMEM)
    hbm = pl.BlockSpec(memory_space=pltpu.HBM)
    dma = pltpu.SemaphoreType.DMA
    blocks = [pltpu.VMEM((N_INTRA, rows, EDIM), BF16) for rows in ROWS]
    return pl.pallas_call(
        kernel,
        out_shape=jax.ShapeDtypeStruct((SD, N_TOWER * QV, EDIM), BF16),
        in_specs=[hbm] * 8,
        out_specs=vmem,
        scratch_shapes=[
            *blocks,
            *blocks,
            pltpu.SMEM((SAMPLES,), jnp.int32),
            pltpu.SMEM((1, TOW_DEV * TFEAT), jnp.int32),
            pltpu.VMEM((TOW_DEV, HID), F32),
            pltpu.VMEM((TOW_DEV, TOUT), F32),
            pltpu.VMEM((N_TOWER * QV, EDIM), BF16),
            pltpu.VMEM((SAMPLES, EDIM), BF16),
            pltpu.VMEM((SAMPLES, EDIM), F32),
            pltpu.VMEM((TOW_DEV, TIN, HID), BF16),
            pltpu.VMEM((TOW_DEV, HID, TOUT), BF16),
            pltpu.VMEM((max(ROWS), EDIM), F32),
            pltpu.VMEM((TOW_DEV, max(ROWS), TIN), BF16),
            pltpu.VMEM((TOW_DEV, max(ROWS), HID), BF16),
            pltpu.VMEM((N_TOWER, QV * SD, EDIM), BF16),
            pltpu.VMEM((N_TOWER, QV * SD, EDIM), BF16),
            pltpu.VMEM((N_TOWER * QV * SD, EDIM), F32),
            pltpu.VMEM((SD, N_TOWER * QV, EDIM), F32),
            pltpu.VMEM((N_TOWER * QV, EDIM), F32),
            dma((EMB_PARTS,)),
            dma,
            dma((6,)),
            dma((NCH,)),
            dma((NCH,)),
            dma,
            dma,
        ],
        compiler_params=pltpu.CompilerParams(
            collective_id=0, has_side_effects=True, vmem_limit_bytes=67043328
        ),
        name="towers",
    )(
        sample_owner,
        feature_assign,
        embeddings,
        first_weight,
        first_bias,
        tower_weight,
        tower_bias,
        proj_weight,
    )


def solution(mesh):
    return jax.shard_map(
        shards,
        mesh=mesh,
        in_specs=(
            P(None, ("tower", "intra")),
            P("tower", None),
            P(),
            P("tower", None, None),
            P("tower", None),
            P("tower", None, None),
            P("tower", None),
            P(),
        ),
        out_specs=P(("tower", "intra"), None, None),
        check_vma=False,
    )
```

time: 94 us -> 86.1 us (0.916); the launches traced: 92.5 us -> 85.9 us
  local copies, waits for them, and re-layouts: 7.07 us -> 1.67 us
  Pallas kernels: 85.4 us -> 84.2 us
    unnamed x15 -> x1, local copies, waits for them, and re-layouts: 7.07 us -> 1.67 us
    pallas_call x1, Pallas kernels: 85.4 us -> 84.2 us  [shards(): pl.pallas_call(kernel, out_shape=jax.ShapeDtypeStruct((SD, N_TOWER * QV,...]
where the time goes in v2:
time: 86.1 us; the launch traced here: 85.9 us
  Pallas kernels  84.2 us (98%)
  local copies, waits for them, and re-layouts  1.67 us (2%)
    pallas_call x1, Pallas kernels, shards(): pl.pallas_call(kernel, out_shape=jax.ShapeDtypeStruct((SD, N_TOWER * QV,...  84.2 us

profile of v2, /device:TPU:1, one launch (start us, length us, event | category | flops | bytes accessed | tf_op | source)
XLA Modules:
  0.0 85.9 jit_solution(2580131778231899079)
XLA Ops:
  0.0 84.2 %towers.1 = bf16[8,128,128]{2,1,0:T(8,128)(2,1)} custom-call(s32[8192]{0:T(1024)} %owner_hbm.1, s32[1,32]{1,0:T(1,128)} %assign_hbm.1, bf16[8192,128]{1,0:T(8,128)(2,1)} %emb_hbm.1, bf16[2,2048,1024]{2,1,0:T(8,128)(2,1)} %w1_hbm.1, f32[2,1024]{1,0:T(2,128)} %b1_hbm.1, bf16[2,1024,256]{2,1,0:T(8,128)(2,1)} %w2_hbm.1, f32[2,256]{1,0:T(2,128)} %b2_hbm.1, ...), custom_call_target="tpu_custom_call" | custom-call | tf_op jit(solution)/shard_map/towers/pallas_call | solution.py:235
  84.2 1.7 %copy.10 = bf16[8,128,128]{2,1,0:T(8,128)(2,1)} copy(bf16[8,128,128]{2,1,0:T(8,128)(2,1)} %towers.1) | data formatting | bytes 524288

commit v3 on v2

--- a/solution.py
+++ b/solution.py
@@ -22,7 +22,7 @@
 ROWS = tuple(len(offsets) * RUN * SD for offsets in CHUNKS)
 FIRST = tuple(RUN * sum(len(offsets) for offsets in CHUNKS[:c]) for c in range(NCH))
 EMB_PARTS = 4
-AHEAD = 16
+EAGER = 2
 MESH = pl.DeviceIdType.MESH
 BF16 = jnp.bfloat16
 F32 = jnp.float32
@@ -34,7 +34,7 @@
     stage, recv = scratch[:NCH], scratch[NCH : 2 * NCH]
     (
         owner, assign, b1, b2, proj, emb_b, emb_f, w1, w2, rows_f, x, hid, send, own, own_f, out_f, proj_f,
-        emb_sem, table_sem, w_sem, send_sem, recv_sem, send2_sem, recv2_sem,
+        emb_sem, table_sem, w_sem, send_sem, recv_sem, send2_sem, recv2_sem, ready, ready2,
     ) = scratch[2 * NCH :]
     tower = lax.axis_index("tower")
     me = lax.axis_index("intra")
@@ -66,14 +66,39 @@
     def y_step(dx, step):
         return (step % 2) * (2 - step) + (step // 2) * (1 - step % 2) * (2 - 4 * (dx % 2))
 
-    @pl.loop(1, N_INTRA)
-    def _(k):
-        pl.semaphore_signal(
-            barrier, inc=1, device_id={"intra": lax.rem(me + k, N_INTRA)}, device_id_type=MESH
-        )
+    def member(order):
+        return tx, (y % RUN) + RUN * ((order // 2) % 2), order // 4, order % 2
+
+    def source_of(k):
         dx = k // RUN
-        sender = place((tx + 8 - dx) % 8, (y + 8 - y_step(dx, k % RUN)) % 8, z, core)
-        pl.semaphore_signal(barrier, inc=1, device_id=sender, device_id_type=MESH)
+        return (tx + 8 - dx) % 8, (y + 8 - y_step(dx, k % RUN)) % 8
+
+    def target_of(dx, dy):
+        return (tx + dx) % 8, (y + 8 + dy) % 8
+
+    order = z * 4 + (y // RUN) * 2 + core
+    rank = y * 8 + tx
+
+    @pl.loop(order + 1, N_INTRA)
+    def _(later):
+        pl.semaphore_signal(barrier, inc=1, device_id=place(*member(later)), device_id_type=MESH)
+
+    def greet(k, count):
+        sx, sy = source_of(k)
+        gx, gy = target_of(k // RUN, y_step(k // RUN, k % RUN))
+
+        @pl.when(sy * 8 + sx > rank)
+        def _():
+            pl.semaphore_signal(barrier, inc=1, device_id=place(sx, sy, z, core), device_id_type=MESH)
+
+        @pl.when(gy * 8 + gx > rank)
+        def _():
+            pl.semaphore_signal(barrier, inc=1, device_id=place(gx, gy, z, core), device_id_type=MESH)
+
+        count = count + jnp.where(sy * 8 + sx < rank, 1, 0)
+        return count + jnp.where(gy * 8 + gx < rank, 1, 0)
+
+    earlier = lax.fori_loop(1, N_TOWER, greet, order)
 
     for i, copy in enumerate(emb_copies):
         copy.wait()
@@ -103,43 +128,69 @@
                 rows_f[pl.ds(pos * SD + r, 1), :] = emb_f[pl.ds(owner[base + r], 1), :]
         return rows_f[pl.ds(0, rows), :].astype(BF16)
 
-    for c in range(NCH):
+    @pl.when(earlier > 0)
+    def _():
+        pl.semaphore_wait(barrier, earlier)
+
+    @pl.loop(0, order)
+    def _(sooner):
+        pl.semaphore_signal(ready.at[me], inc=1, device_id=place(*member(sooner)), device_id_type=MESH)
+
+    @pl.loop(1, N_TOWER)
+    def _(k):
+        sx, sy = source_of(k)
+
+        @pl.when(sy * 8 + sx < rank)
+        def _():
+            pl.semaphore_signal(
+                ready2.at[k], inc=1, device_id=place(sx, sy, z, core), device_id_type=MESH
+            )
+
+    def copy_of(c, slot, peer):
+        return pltpu.make_async_remote_copy(
+            src_ref=stage[c].at[slot],
+            dst_ref=recv[c].at[me],
+            send_sem=send_sem.at[c],
+            recv_sem=recv_sem.at[c],
+            device_id=place(*peer),
+            device_id_type=MESH,
+        )
+
+    @pl.loop(0, N_INTRA)
+    def _(k):
+        level = k // 4
+        down = jnp.where(level < z, 1, 0)
+        at = (down * (z - 1 - level) + (1 - down) * level) * 4 + k % 4
+        peer = member(at)
+
+        @pl.when(at != order)
+        def _():
+            for c in range(EAGER):
+                stage[c][k] = gather(steps_of(c), peer)
+
+            @pl.when(at > order)
+            def _():
+                pl.semaphore_wait(ready.at[place(*peer)["intra"]], 1)
+
+            for c in range(EAGER):
+                copy_of(c, k, peer).start()
+
+    for c in range(EAGER):
+        recv[c][me] = gather(steps_of(c), (tx, y, z, core))
+
+    for c in range(EAGER, NCH):
         steps = steps_of(c)
 
-        def copy_of(k, c=c):
-            return pltpu.make_async_remote_copy(
-                src_ref=stage[c].at[k],
-                dst_ref=recv[c].at[me],
-                send_sem=send_sem.at[c],
-                recv_sem=recv_sem.at[c],
-                device_id=place(*peer_of(k)),
-                device_id_type=MESH,
-            )
-
-        if c == 0:
-
-            @pl.loop(0, AHEAD)
-            def _(k, steps=steps):
-                stage[0][k] = gather(steps, peer_of(k))
-
-            pl.semaphore_wait(barrier, (N_INTRA - 1) + (N_TOWER - 1))
-
-            @pl.loop(0, AHEAD - 1)
-            def _(k, copy_of=copy_of):
-                copy_of(k).start()
-
-        begin = AHEAD if c == 0 else 0
-
-        @pl.loop(begin, N_INTRA - 1)
-        def _(k, c=c, steps=steps, copy_of=copy_of):
+        @pl.loop(0, N_INTRA - 1)
+        def _(k, c=c, steps=steps):
             stage[c][k] = gather(steps, peer_of(k))
 
             @pl.when(k > 0)
             def _():
-                copy_of(k - 1).start()
+                copy_of(c, k - 1, peer_of(k - 1)).start()
 
         recv[c][me] = gather(steps, (tx, y, z, core))
-        copy_of(N_INTRA - 2).start()
+        copy_of(c, N_INTRA - 2, peer_of(N_INTRA - 2)).start()
 
     for copy in w_copies:
         copy.wait()
@@ -184,10 +235,19 @@
                     dst_ref=own.at[tower],
                     send_sem=send2_sem,
                     recv_sem=recv2_sem,
-                    device_id=place((tx + dx) % 8, (y + 8 + dy) % 8, z, core),
+                    device_id=place(*target_of(dx, dy), z, core),
                     device_id_type=MESH,
                 )
             )
+        for pos, (dx, dy) in enumerate(steps):
+            if dx == 0 and pos % RUN == 0:
+                continue
+            gx, gy = target_of(dx, dy)
+
+            @pl.when(gy * 8 + gx > rank)
+            def _(dx=dx, pos=pos):
+                pl.semaphore_wait(ready2.at[dx * RUN + pos % RUN], 1)
+
         for copy in copies:
             copy.start()
 
@@ -264,6 +324,8 @@
             dma((NCH,)),
             dma,
             dma,
+            pltpu.SemaphoreType.REGULAR((N_INTRA,)),
+            pltpu.SemaphoreType.REGULAR((N_TOWER,)),
         ],
         compiler_params=pltpu.CompilerParams(
             collective_id=0, has_side_effects=True, vmem_limit_bytes=67043328

time: 86.1 us -> 96.5 us (1.12)
  Pallas kernels: 84.2 us -> 94.6 us
    pallas_call x1, Pallas kernels: 84.2 us -> 94.6 us  [shards(): pl.pallas_call(kernel, out_shape=jax.ShapeDtypeStruct((SD, N_TOWER * QV,...]
where the time goes in v3:
time: 96.5 us; the launch traced here: 96.3 us
  Pallas kernels  94.6 us (98%)
  local copies, waits for them, and re-layouts  1.67 us (2%)
    pallas_call x1, Pallas kernels, shards(): pl.pallas_call(kernel, out_shape=jax.ShapeDtypeStruct((SD, N_TOWER * QV,...  94.6 us

profile of v3, /device:TPU:1, one launch (start us, length us, event | category | flops | bytes accessed | tf_op | source)
XLA Modules:
  0.0 96.3 jit_solution(13485923574956626755)
XLA Ops:
  0.0 94.6 %towers.1 = bf16[8,128,128]{2,1,0:T(8,128)(2,1)} custom-call(s32[8192]{0:T(1024)} %owner_hbm.1, s32[1,32]{1,0:T(1,128)} %assign_hbm.1, bf16[8192,128]{1,0:T(8,128)(2,1)} %emb_hbm.1, bf16[2,2048,1024]{2,1,0:T(8,128)(2,1)} %w1_hbm.1, f32[2,1024]{1,0:T(2,128)} %b1_hbm.1, bf16[2,1024,256]{2,1,0:T(8,128)(2,1)} %w2_hbm.1, f32[2,256]{1,0:T(2,128)} %b2_hbm.1, ...), custom_call_target="tpu_custom_call" | custom-call | tf_op jit(solution)/shard_map/towers/pallas_call | solution.py:295
  94.7 1.7 %copy.10 = bf16[8,128,128]{2,1,0:T(8,128)(2,1)} copy(bf16[8,128,128]{2,1,0:T(8,128)(2,1)} %towers.1) | data formatting | bytes 524288

commit v4 on v3

--- a/solution.py
+++ b/solution.py
@@ -22,7 +22,6 @@
 ROWS = tuple(len(offsets) * RUN * SD for offsets in CHUNKS)
 FIRST = tuple(RUN * sum(len(offsets) for offsets in CHUNKS[:c]) for c in range(NCH))
 EMB_PARTS = 4
-EAGER = 2
 MESH = pl.DeviceIdType.MESH
 BF16 = jnp.bfloat16
 F32 = jnp.float32
@@ -156,29 +155,36 @@
             device_id_type=MESH,
         )
 
-    @pl.loop(0, N_INTRA)
-    def _(k):
-        level = k // 4
-        down = jnp.where(level < z, 1, 0)
-        at = (down * (z - 1 - level) + (1 - down) * level) * 4 + k % 4
-        peer = member(at)
-
-        @pl.when(at != order)
+    def order_of(peer):
+        return peer[2] * 4 + (peer[1] // RUN) * 2 + peer[3]
+
+    def send_first(at):
+        copy_of(0, at, member(at)).start()
+
+    def first(k, before):
+        peer = peer_of(k)
+        at = order_of(peer)
+        stage[0][at] = gather(steps_of(0), peer)
+
+        @pl.when(before < order)
         def _():
-            for c in range(EAGER):
-                stage[c][k] = gather(steps_of(c), peer)
-
-            @pl.when(at > order)
-            def _():
-                pl.semaphore_wait(ready.at[place(*peer)["intra"]], 1)
-
-            for c in range(EAGER):
-                copy_of(c, k, peer).start()
-
-    for c in range(EAGER):
-        recv[c][me] = gather(steps_of(c), (tx, y, z, core))
-
-    for c in range(EAGER, NCH):
+            send_first(before)
+
+        return at
+
+    last = lax.fori_loop(0, N_INTRA - 1, first, order)
+    recv[0][me] = gather(steps_of(0), (tx, y, z, core))
+
+    @pl.when(last < order)
+    def _():
+        send_first(last)
+
+    @pl.loop(order + 1, N_INTRA)
+    def _(at):
+        pl.semaphore_wait(ready.at[place(*member(at))["intra"]], 1)
+        send_first(at)
+
+    for c in range(1, NCH):
         steps = steps_of(c)
 
         @pl.loop(0, N_INTRA - 1)

time: 96.5 us -> 87.2 us (0.904)
  Pallas kernels: 94.6 us -> 85.4 us
    pallas_call x1, Pallas kernels: 94.6 us -> 85.4 us  [shards(): pl.pallas_call(kernel, out_shape=jax.ShapeDtypeStruct((SD, N_TOWER * QV,...]
where the time goes in v4:
time: 87.2 us; the launch traced here: 87.1 us
  Pallas kernels  85.4 us (98%)
  local copies, waits for them, and re-layouts  1.67 us (2%)
    pallas_call x1, Pallas kernels, shards(): pl.pallas_call(kernel, out_shape=jax.ShapeDtypeStruct((SD, N_TOWER * QV,...  85.4 us

profile of v4, /device:TPU:1, one launch (start us, length us, event | category | flops | bytes accessed | tf_op | source)
XLA Modules:
  0.0 87.1 jit_solution(2397062590095651253)
XLA Ops:
  0.0 85.4 %towers.1 = bf16[8,128,128]{2,1,0:T(8,128)(2,1)} custom-call(s32[8192]{0:T(1024)} %owner_hbm.1, s32[1,32]{1,0:T(1,128)} %assign_hbm.1, bf16[8192,128]{1,0:T(8,128)(2,1)} %emb_hbm.1, bf16[2,2048,1024]{2,1,0:T(8,128)(2,1)} %w1_hbm.1, f32[2,1024]{1,0:T(2,128)} %b1_hbm.1, bf16[2,1024,256]{2,1,0:T(8,128)(2,1)} %w2_hbm.1, f32[2,256]{1,0:T(2,128)} %b2_hbm.1, ...), custom_call_target="tpu_custom_call" | custom-call | tf_op jit(solution)/shard_map/towers/pallas_call | solution.py:301
  85.4 1.7 %copy.10 = bf16[8,128,128]{2,1,0:T(8,128)(2,1)} copy(bf16[8,128,128]{2,1,0:T(8,128)(2,1)} %towers.1) | data formatting | bytes 524288
